TPU v7x, 32 devices: a whole 2x2x4 slice. The times are simulated.
32 devices in a mesh: circ: 4 (over y, x), span: 8 (over z, core).
Axes of the slice: x: 2, y: 2, z: 4, core: 2. Of those that a mesh axis runs over, the one named last changes fastest.
Arguments:
- elem_rows: bfloat16 [80, 24576], P(None, ('circ', 'span')), may hold values from -6 to 6
- coupling: bfloat16 [24, 80, 80, 1024], P('circ', None, None, 'span')
- inverses: bfloat16 [24, 80, 80, 1024], P('circ', None, None, 'span'), may hold values from -0.625 to 0.625
- send_rows: int32 [32, 32, 48], P(('circ', 'span')), may hold values from 0 to 767, as said below
- recv_cells: int32 [32, 32, 48], P(('circ', 'span')), may hold values from 0 to 767, as said below
- slot_counts: int32 [32, 32], P(('circ', 'span')), may hold values from 0 to 48, as said below
Outputs:
- corrections: float32 [80, 24576], P(None, ('circ', 'span'))
Inputs may be any that keep to these rules, and one draw needn't show every extreme that they name: `send_rows`: each source's filled slots name each of its 768 rows exactly once, each owner's filled slots name each of its 768 cells exactly once; unfilled slots hold 0. `recv_cells`: as send_rows, for the owners' cells. `slot_counts`: every owner's counts sum to 768, and so do every source's; some pair fills all 48 slots.
All inputs are finite; a program needn't handle non-finite values.
Results may differ from a plain program's by a relative error of at most 0.0003.
Values may be sent and summed in bfloat16 or wider, within the bound.
A program may use at most 128 MiB of HBM per device.

v0:
```python
import functools

import jax
import jax.numpy as jnp
from jax import lax
from jax.experimental import pallas as pl
from jax.experimental.pallas import tpu as pltpu
from jax.sharding import PartitionSpec as P

MESH = pl.DeviceIdType.MESH


def merge(low, high, half, mask):
    if 2 * half == low.shape[0]:
        return jnp.where(mask, low, high) + pltpu.roll(jnp.where(mask, high, low), half, axis=0)
    back = low.shape[0] - half
    return jnp.where(mask, low + pltpu.roll(low, back, axis=0), high + pltpu.roll(high, half, axis=0))


def fold(parts):
    row = lax.broadcasted_iota(jnp.int32, parts[0].shape, 0)
    half = len(parts) // 2
    while half:
        mask = (row & half) == 0
        parts = [merge(parts[i], parts[i + half], half, mask) for i in range(half)]
        half //= 2
    return parts[0]


def block_rows(mat_ref, position, base, vector):
    width = vector.shape[0]
    parts = []
    for i in range(8):
        total = None
        for start in range(0, width, 16):
            piece = mat_ref[position, base + i, start : start + 16, :]
            term = piece.astype(jnp.float32) * vector[start : start + 16]
            total = term if total is None else total + term
        parts.append(total[:8] + total[8:])
    return fold(parts)


def relay_kernel(
    n_circ, rows_ref, inv_hbm, coup_hbm, out_ref, inv, coup, forcing, state, inbox, outbox, inv_sem, coup_sem, send_sem, recv_sem
):
    me = lax.axis_index("circ")
    right, left = lax.rem(me + 1, n_circ), lax.rem(me + n_circ - 1, n_circ)
    segment, width = coup.shape[0], coup.shape[1]
    blocks = width // 8

    loads = [pltpu.make_async_copy(inv_hbm.at[k], inv.at[k], inv_sem.at[k]) for k in range(segment)]
    loads += [pltpu.make_async_copy(coup_hbm.at[k], coup.at[k], coup_sem.at[k]) for k in range(segment)]
    for load in loads:
        load.start()

    barrier = pltpu.get_barrier_semaphore()
    for neighbour in (left, right):
        pl.semaphore_signal(barrier, inc=1, device_id={"circ": neighbour}, device_id_type=MESH)
    pl.semaphore_wait(barrier, 2)

    for k in range(segment):
        loads[k].wait()
        vector = rows_ref[k].astype(jnp.float32)

        def force(b, _, k=k, vector=vector):
            base = pl.multiple_of(b * 8, 8)
            forcing[k, pl.ds(base, 8), :] = block_rows(inv, k, base, vector)
            return 0

        lax.fori_loop(0, blocks, force, 0)
    for k in range(segment):
        loads[segment + k].wait()

    def hop(turn, slot):
        return pltpu.make_async_remote_copy(
            src_ref=outbox.at[turn],
            dst_ref=inbox.at[slot],
            send_sem=send_sem.at[turn],
            recv_sem=recv_sem.at[slot],
            device_id={"circ": right},
            device_id_type=MESH,
        )

    def sweep(target):
        def step(k, _):
            vector = state[...]

            def advance(b, _):
                base = pl.multiple_of(b * 8, 8)
                value = forcing[k, pl.ds(base, 8), :] + block_rows(coup, k, base, vector)
                state[pl.ds(base, 8), :] = value
                if target is not None:
                    target[k, pl.ds(base, 8), :] = value
                return 0

            lax.fori_loop(0, blocks, advance, 0)
            return 0

        lax.fori_loop(0, segment, step, 0)

    @pl.when(me == 0)
    def _():
        state[...] = jnp.zeros_like(state)

    @pl.when(me > 0)
    def _():
        hop(0, 0).wait_recv()
        state[...] = inbox[0]

    sweep(None)
    outbox[0] = state[...]
    slot = jnp.where(me == n_circ - 1, 1, 0)
    first = hop(0, slot)
    first.start()
    hop(0, 1).wait_recv()
    state[...] = inbox[1]
    sweep(out_ref)

    @pl.when(me < n_circ - 1)
    def _():
        outbox[1] = state[...]
        second = hop(1, 1)
        second.start()
        second.wait_send()

    first.wait_send()


def relay(rows, inverses, coupling):
    segment, width, _, lines = coupling.shape
    n_circ = lax.axis_size("circ")
    state = pltpu.VMEM((width, lines), jnp.float32)
    boxes = pltpu.VMEM((2, width, lines), jnp.float32)
    return pl.pallas_call(
        functools.partial(relay_kernel, n_circ),
        out_shape=jax.ShapeDtypeStruct((segment, width, lines), jnp.float32),
        in_specs=[
            pl.BlockSpec(memory_space=pltpu.VMEM),
            pl.BlockSpec(memory_space=pl.ANY),
            pl.BlockSpec(memory_space=pl.ANY),
        ],
        out_specs=pl.BlockSpec(memory_space=pltpu.VMEM),
        scratch_shapes=[
            pltpu.VMEM(inverses.shape, jnp.bfloat16),
            pltpu.VMEM(coupling.shape, jnp.bfloat16),
            pltpu.VMEM((segment, width, lines), jnp.float32),
            state,
            boxes,
            boxes,
            pltpu.SemaphoreType.DMA((segment,)),
            pltpu.SemaphoreType.DMA((segment,)),
            pltpu.SemaphoreType.DMA((2,)),
            pltpu.SemaphoreType.DMA((2,)),
        ],
        compiler_params=pltpu.CompilerParams(
            collective_id=0, has_side_effects=True, vmem_limit_bytes=48 * 1024 * 1024
        ),
        name="relay",
    )(rows, inverses, coupling)


def staged(elem_rows, coupling, inverses, send_rows, recv_cells, slot_counts):
    features, cell_count = elem_rows.shape
    peer_count, slot_count = (send_rows.shape[1], send_rows.shape[2])
    segment, line_count = (coupling.shape[0], coupling.shape[3])
    outgoing = jnp.take(elem_rows, send_rows[0].reshape(-1), axis=1).reshape(
        features, peer_count, slot_count
    )
    arrived = lax.all_to_all(outgoing, ("circ", "span"), split_axis=1, concat_axis=1, tiled=True)
    filled = jnp.arange(slot_count, dtype=jnp.int32)[None, :] < slot_counts[0][:, None]
    targets = jnp.where(filled, recv_cells[0], cell_count).reshape(-1)
    line_rows = (
        jnp.zeros((features, cell_count), jnp.bfloat16)
        .at[:, targets]
        .set(arrived.reshape(features, -1), mode="drop")
    )
    line_cells = jnp.transpose(line_rows.reshape(features, segment, line_count), (1, 0, 2))
    states = relay(line_cells, inverses, coupling)
    solved = jnp.transpose(states, (1, 0, 2)).reshape(features, cell_count)
    returning = jnp.take(solved, recv_cells[0].reshape(-1), axis=1).reshape(
        features, peer_count, slot_count
    )
    returning = jnp.where(filled[None, :, :], returning, 0.0)
    returned = lax.all_to_all(returning, ("circ", "span"), split_axis=1, concat_axis=1, tiled=True)
    return (
        jnp.zeros((features, cell_count), jnp.float32)
        .at[:, send_rows[0].reshape(-1)]
        .add(returned.reshape(features, -1))
    )


def code(values, lane, width, extra):
    size = jnp.abs(values)
    tiny = jnp.float32(1e-36)
    top_main = jnp.max(jnp.where(lane < width, size, tiny), axis=1, keepdims=True)
    top_extra = jnp.max(jnp.where(lane < width, tiny, size), axis=1, keepdims=True)
    power_main = jnp.ceil(jnp.log2(jnp.maximum(top_main, tiny)))
    power_extra = jnp.ceil(jnp.log2(jnp.maximum(top_extra, tiny)))
    root = jnp.exp2(-0.5 * jnp.where(lane < width, power_main, power_extra))
    whole = jnp.round(values * root * root * 32000.0)
    whole = jnp.where(lane == width + extra, power_main, whole)
    whole = jnp.where(lane == width + extra + 1, power_extra, whole)
    return whole.astype(jnp.int32).astype(jnp.int16)


def decode(coded, lane, width, extra):
    whole = coded.astype(jnp.int32).astype(jnp.float32)
    power_main = jnp.sum(jnp.where(lane == width + extra, whole, 0.0), axis=1, keepdims=True)
    power_extra = jnp.sum(jnp.where(lane == width + extra + 1, whole, 0.0), axis=1, keepdims=True)
    root = jnp.exp2(0.5 * jnp.where(lane < width, power_main, power_extra))
    return jnp.where(lane < width + extra, whole * (1.0 / 32000.0) * root * root, 0.0)


def split(values):
    high = values.astype(jnp.bfloat16)
    return high, (values - high.astype(jnp.float32)).astype(jnp.bfloat16)


def nt(a, b):
    return lax.dot_general(a, b, (((1,), (1,)), ((), ())), preferred_element_type=jnp.float32)


def nn(a, b):
    return jnp.dot(a, b, preferred_element_type=jnp.float32)


def spread(table):
    width, cells = table.shape
    half = width // 2
    head = jnp.zeros((width, cells), jnp.float32)
    tail = jnp.zeros((128 - width - half, cells), jnp.float32)
    return (
        jnp.concatenate([table, jnp.zeros((128 - width, cells), jnp.float32)], axis=0),
        jnp.concatenate([head, table[:half], tail], axis=0),
        jnp.concatenate([head, table[half:], tail], axis=0),
    )


def fused_kernel(
    n_circ, n_span, elem_ref, send_ref, recv_ref, count_ref, inv_hbm, coup_hbm, out_ref,
    inv, coup, wide, line_rows, forcing, solved, state, inbox, pick_send, pick_recv, sent, arrived, back_sent, back_arrived,
    inv_sem, coup_sem, send_sem, recv_sem, go_send, go_recv, back_send, back_recv,
):
    circ, span = lax.axis_index("circ"), lax.axis_index("span")
    peers = n_circ * n_span
    me = circ * n_span + span
    right = lax.rem(circ + 1, n_circ)
    segment, width, lines = forcing.shape
    cells = segment * lines
    third = sent.shape[1] // 2
    half = width // 2
    blocks = width // 8

    coup_loads = [pltpu.make_async_copy(coup_hbm.at[k], coup.at[k], coup_sem.at[k]) for k in range(segment)]
    inv_loads = [pltpu.make_async_copy(inv_hbm.at[k], inv.at[k], inv_sem.at[k]) for k in range(segment)]
    for load in coup_loads + inv_loads:
        load.start()

    barrier = pltpu.get_barrier_semaphore()

    def greet(o, _):
        peer = lax.rem(me + o, peers)
        pl.semaphore_signal(
            barrier, inc=1, device_id={"circ": peer // n_span, "span": peer % n_span}, device_id_type=MESH
        )
        return 0

    lax.fori_loop(1, peers, greet, 0)

    def build(index_ref, pick, masked):
        lane = lax.broadcasted_iota(jnp.int32, (third, index_ref.shape[1]), 1)
        slot = lax.broadcasted_iota(jnp.int32, (third, index_ref.shape[1]), 0)
        number = lax.broadcasted_iota(jnp.int32, (third, cells), 1).astype(jnp.float32)
        owner = lax.broadcasted_iota(jnp.int32, count_ref.shape, 1)
        rank = lax.broadcasted_iota(jnp.int32, (third, 1), 0).astype(jnp.float32)

        def one(p, _):
            row = index_ref[pl.ds(p, 1), :].astype(jnp.float32)
            if masked:
                counts = count_ref[...].astype(jnp.float32)
                count = jnp.sum(jnp.where(owner == p, counts, 0.0), axis=1, keepdims=True)
            for t in range(3):
                column = jnp.sum(jnp.where(lane == slot + t * third, row, 0.0), axis=1, keepdims=True)
                if masked:
                    column = jnp.where(rank + float(t * third) < count, column, -1.0)
                hot = jnp.where(number == column, 1.0, 0.0).astype(jnp.bfloat16)
                pick[t, pl.ds(pl.multiple_of(p * third, third), third), :] = hot
            return 0

        lax.fori_loop(0, peers, one, 0)

    def exchange(outs, ins, outs_sem, ins_sem):
        def copy(peer, landing):
            return pltpu.make_async_remote_copy(
                src_ref=outs.at[peer],
                dst_ref=ins.at[landing],
                send_sem=outs_sem.at[peer],
                recv_sem=ins_sem.at[landing],
                device_id={"circ": peer // n_span, "span": peer % n_span},
                device_id_type=MESH,
            )

        def start(o, _):
            copy(lax.rem(me + o, peers), me).start()
            return 0

        def land(o, _):
            peer = lax.rem(me + peers - o, peers)
            copy(peer, peer).wait_recv()
            return 0

        def drain(o, _):
            copy(lax.rem(me + o, peers), me).wait_send()
            return 0

        return (
            lambda: lax.fori_loop(1, peers, start, 0),
            lambda: lax.fori_loop(1, peers, land, 0),
            lambda: lax.fori_loop(1, peers, drain, 0),
        )

    build(send_ref, pick_send, False)
    whole, low, high = [w.astype(jnp.bfloat16) for w in spread(elem_ref[...].astype(jnp.float32))]
    first = nt(pick_send[0], whole) + nt(pick_send[2], low)
    second = nt(pick_send[1], whole) + nt(pick_send[2], high)
    sent[:, :third, :] = first.astype(jnp.bfloat16).reshape(peers, third, 128)
    sent[:, third:, :] = second.astype(jnp.bfloat16).reshape(peers, third, 128)

    pl.semaphore_wait(barrier, peers - 1)
    start, land, drain_go = exchange(sent, arrived, go_send, go_recv)
    start()
    arrived[me] = sent[me]
    build(recv_ref, pick_recv, True)
    for k in range(segment):
        coup_loads[k].wait()

        def widen(b, _, k=k):
            for i in range(8):
                wide[k, b * 8 + i] = coup[k, b * 8 + i].astype(jnp.float32)
            return 0

        lax.fori_loop(0, blocks, widen, 0)
    land()

    def turned(block):
        return jnp.transpose(block.reshape(peers * third, 128).astype(jnp.float32))

    first, second = turned(arrived[:, :third, :]), turned(arrived[:, third:, :])

    def collect(first, second, pick):
        extra = jnp.concatenate([first[width : width + half], second[width : width + half]], axis=0)
        parts = [first[:width], second[:width], extra]
        return parts, pick

    parts, _ = collect(first, second, pick_recv)
    line = sum(nn(parts[t].astype(jnp.bfloat16), pick_recv[t]) for t in range(3))

    for k in range(segment):
        line_rows[k] = line[:, k * lines : (k + 1) * lines].astype(jnp.bfloat16)
    for k in range(segment):
        inv_loads[k].wait()
        vector = line_rows[k].astype(jnp.float32)

        def force(b, _, k=k, vector=vector):
            base = pl.multiple_of(b * 8, 8)
            forcing[k, pl.ds(base, 8), :] = block_rows(inv, k, base, vector)
            return 0

        lax.fori_loop(0, blocks, force, 0)

    cut = (blocks // 4) * 16
    chunks = ((0, cut), (cut, width))

    def hop(turn, slot, chunk):
        rows = pl.ds(chunks[chunk][0], chunks[chunk][1] - chunks[chunk][0])
        return pltpu.make_async_remote_copy(
            src_ref=solved.at[segment - 1, rows],
            dst_ref=inbox.at[slot, rows],
            send_sem=send_sem.at[turn, chunk],
            recv_sem=recv_sem.at[slot, chunk],
            device_id={"circ": right},
            device_id_type=MESH,
        )

    def sweep(emit):
        for k in range(segment):
            vector = state[...] if k == 0 else solved[k - 1]

            def advance(b, _, k=k, vector=vector):
                for base in (pl.multiple_of(b * 16, 16), pl.multiple_of(b * 16 + 8, 8)):
                    rows = block_rows(wide, k, base, vector)
                    solved[k, pl.ds(base, 8), :] = forcing[k, pl.ds(base, 8), :] + rows
                return 0

            if k < segment - 1:
                lax.fori_loop(0, blocks // 2, advance, 0)
            else:
                for chunk in range(2):
                    lax.fori_loop(chunks[chunk][0] // 16, chunks[chunk][1] // 16, advance, 0)
                    emit(chunk)

    @pl.when(circ == 0)
    def _():
        state[...] = jnp.zeros_like(state)

    @pl.when(circ > 0)
    def _():
        for chunk in range(2):
            hop(0, 0, chunk).wait_recv()
        state[...] = inbox[0]

    landing = jnp.where(circ == n_circ - 1, 1, 0)
    sweep(lambda chunk: hop(0, landing, chunk).start())
    for chunk in range(2):
        hop(0, 1, chunk).wait_send()
    for chunk in range(2):
        hop(0, 1, chunk).wait_recv()
    state[...] = inbox[1]

    def last(chunk):
        @pl.when(circ < n_circ - 1)
        def _():
            hop(1, 1, chunk).start()

    sweep(last)

    table = jnp.concatenate([solved[k] for k in range(segment)], axis=1)
    whole, low, high = [jnp.concatenate(split(w), axis=0) for w in spread(table)]

    def both(picked):
        return picked[:, :128] + picked[:, 128:]

    lane = lax.broadcasted_iota(jnp.int32, (peers * third, 128), 1)
    first = both(nt(pick_recv[0], whole) + nt(pick_recv[2], low))
    second = both(nt(pick_recv[1], whole) + nt(pick_recv[2], high))
    back_sent[:, :third, :] = code(first, lane, width, half).reshape(peers, third, 128)
    back_sent[:, third:, :] = code(second, lane, width, half).reshape(peers, third, 128)
    start, land, drain_back = exchange(back_sent, back_arrived, back_send, back_recv)
    start()
    back_arrived[me] = back_sent[me]
    land()

    def opened(block):
        return jnp.transpose(decode(block.reshape(peers * third, 128), lane, width, half))

    first, second = opened(back_arrived[:, :third, :]), opened(back_arrived[:, third:, :])
    parts, _ = collect(first, second, pick_send)
    total = sum(nn(jnp.concatenate(split(parts[t]), axis=0), pick_send[t]) for t in range(3))
    out_ref[...] = total[:width] + total[width:]

    @pl.when(circ < n_circ - 1)
    def _():
        for chunk in range(2):
            hop(1, 1, chunk).wait_send()

    drain_go()
    drain_back()


def fused(elem_rows, coupling, inverses, send_rows, recv_cells, slot_counts):
    segment, width, _, lines = coupling.shape
    peers, slots = send_rows.shape[1], send_rows.shape[2]
    n_circ, n_span = lax.axis_size("circ"), lax.axis_size("span")
    third = slots // 3
    vmem = pl.BlockSpec(memory_space=pltpu.VMEM)
    hbm = pl.BlockSpec(memory_space=pl.ANY)
    boxes = pltpu.VMEM((2, width, lines), jnp.float32)
    states = pltpu.VMEM((segment, width, lines), jnp.float32)
    pick = pltpu.VMEM((3, peers * third, segment * lines), jnp.bfloat16)
    go = pltpu.VMEM((peers, 2 * third, 128), jnp.bfloat16)
    back = pltpu.VMEM((peers, 2 * third, 128), jnp.int16)
    dma = pltpu.SemaphoreType.DMA
    return pl.pallas_call(
        functools.partial(fused_kernel, n_circ, n_span),
        out_shape=jax.ShapeDtypeStruct(elem_rows.shape, jnp.float32),
        in_specs=[vmem, vmem, vmem, vmem, hbm, hbm],
        out_specs=vmem,
        scratch_shapes=[
            pltpu.VMEM(inverses.shape, jnp.bfloat16),
            pltpu.VMEM(coupling.shape, jnp.bfloat16),
            pltpu.VMEM(coupling.shape, jnp.float32),
            pltpu.VMEM((segment, width, lines), jnp.bfloat16),
            states,
            states,
            pltpu.VMEM((width, lines), jnp.float32),
            boxes,
            pick,
            pick,
            go,
            go,
            back,
            back,
            dma((segment,)),
            dma((segment,)),
            dma((2, 2)),
            dma((2, 2)),
            dma((peers,)),
            dma((peers,)),
            dma((peers,)),
            dma((peers,)),
        ],
        compiler_params=pltpu.CompilerParams(
            collective_id=1, has_side_effects=True, vmem_limit_bytes=60 * 1024 * 1024
        ),
        name="smooth",
    )(elem_rows, send_rows[0], recv_cells[0], slot_counts, inverses, coupling)


def packs(width, slots, cells, lines):
    return slots % 48 == 0 and width % 16 == 0 and width + width // 2 + 2 <= 128 and lines == 128


def local(*arrays):
    coupling, send_rows = arrays[1], arrays[3]
    if packs(coupling.shape[1], send_rows.shape[2], arrays[0].shape[1], coupling.shape[3]):
        return fused(*arrays)
    return staged(*arrays)


def solution(mesh):
    return jax.shard_map(
        local,
        mesh=mesh,
        in_specs=(
            P(None, ("circ", "span")),
            P("circ", None, None, "span"),
            P("circ", None, None, "span"),
            P(("circ", "span"), None, None),
            P(("circ", "span"), None, None),
            P(("circ", "span"), None),
        ),
        out_specs=P(None, ("circ", "span")),
        check_vma=False,
    )
```

profile of v0, /device:TPU:0, one launch (start us, length us, event | category | flops | bytes accessed | tf_op | source)
XLA Modules:
  0.0 65.5 jit_solution(7018954380085040383)
XLA Ops:
  0.0 63.9 %smooth.1 = f32[80,768]{1,0:T(8,128)} custom-call(bf16[80,768]{1,0:T(8,128)(2,1)} %elem_ref.1, s32[32,48]{1,0:T(8,128)} %bitcast.2, s32[32,48]{1,0:T(8,128)} %bitcast.3, s32[1,32]{1,0:T(1,128)} %count_ref.1, bf16[6,80,80,128]{3,2,1,0:T(8,128)(2,1)} %inv_hbm.1, bf16[6,80,80,128]{3,2,1,0:T(8,128)(2,1)} %coup_hbm.1), custom_call_target="tpu_custom_call" | custom-call | tf_op jit(solution)/shard_map/smooth/pallas_call | solution.py:473
  63.9 1.7 %copy.8 = f32[80,768]{1,0:T(8,128)} copy(f32[80,768]{1,0:T(8,128)} %smooth.1) | data formatting | bytes 491520
where the time goes:
time: 65.7 us; the launch traced here: 65.5 us
  Pallas kernels  63.9 us (97%)
  local copies, waits for them, and re-layouts  1.65 us (3%)
    pallas_call x1, Pallas kernels, fused(): pl.pallas_call(functools.partial(fused_kernel, n_circ, n_span), out_shape...  63.9 us
    unnamed x1, local copies, waits for them, and re-layouts  1.65 us

commit v1 on v0

--- a/solution.py
+++ b/solution.py
@@ -8,6 +8,7 @@
 from jax.sharding import PartitionSpec as P
 
 MESH = pl.DeviceIdType.MESH
+GROUPS = 4
 
 
 def merge(low, high, half, mask):
@@ -236,9 +237,116 @@
     )
 
 
+def turn_lanes(values):
+    count = len(values)
+    lane = lax.broadcasted_iota(jnp.int32, values[0].shape, 1)
+    size = values[0].shape[1]
+    step = count // 2
+    while step:
+        wide = size // count * step
+        upper = (lane & wide) != 0
+        swapped = list(values)
+        for i in range(count):
+            if i & step == 0:
+                low, high = values[i], values[i + step]
+                swapped[i] = jnp.where(upper, pltpu.roll(high, wide, axis=1), low)
+                swapped[i + step] = jnp.where(upper, high, pltpu.roll(low, size - wide, axis=1))
+        values = swapped
+        step //= 2
+    return values
+
+
+def fill_lanes(value, count):
+    size = value.shape[1]
+    lane = lax.broadcasted_iota(jnp.int32, value.shape, 1)
+    values = [value]
+    step = count // 2
+    while step:
+        wide = size // count * step
+        upper = (lane & wide) != 0
+        grown = []
+        for held in values:
+            moved = pltpu.roll(held, wide, axis=1)
+            if 2 * wide != size:
+                back = pltpu.roll(held, size - wide, axis=1)
+            else:
+                back = moved
+            grown += [jnp.where(upper, moved, held), jnp.where(upper, held, back)]
+        values = grown
+        step //= 2
+    return values
+
+
+def halves(tile):
+    low = lax.broadcasted_iota(jnp.int32, tile.shape, 0) < 4
+    moved = pltpu.roll(tile, 4, axis=0)
+    return jnp.where(low, tile, moved), jnp.where(low, moved, tile)
+
+
+def joined(first, second):
+    low = lax.broadcasted_iota(jnp.int32, first.shape, 0) < 4
+    return jnp.where(low, first, second)
+
+
+def row_plan(width, groups):
+    full = width // 8 // groups
+    spare = (width // 8 - full * groups) * 8 // groups
+    return full, spare
+
+
+def to_groups(tiles, groups):
+    full, spare = row_plan(8 * len(tiles), groups)
+    rows = [turn_lanes(tiles[b * groups : (b + 1) * groups]) for b in range(full)]
+    if spare:
+        pieces = [piece for tile in tiles[full * groups :] for piece in halves(tile)]
+        rows.append(turn_lanes(pieces))
+    return [[row[g] for row in rows] for g in range(groups)]
+
+
+def from_groups(packed, width):
+    groups = len(packed)
+    full, spare = row_plan(width, groups)
+    tiles = []
+    for b in range(full):
+        tiles += turn_lanes([packed[g][b] for g in range(groups)])
+    if spare:
+        pieces = turn_lanes([packed[g][full] for g in range(groups)])
+        tiles += [joined(pieces[i], pieces[i + 1]) for i in range(0, groups, 2)]
+    return tiles
+
+
+def replicate(rows, width, groups):
+    full, spare = row_plan(width, groups)
+    tiles = []
+    for b in range(full):
+        tiles += fill_lanes(rows[b], groups)
+    if spare:
+        pieces = fill_lanes(rows[full], groups)
+        tiles += [joined(pieces[i], pieces[i + 1]) for i in range(0, groups, 2)]
+    return tiles
+
+
+def advance(wide, group, position, tiles, add, width, groups):
+    full, spare = row_plan(width, groups)
+    rows = []
+    for b in range(full + (spare > 0)):
+        parts = []
+        for i in range(8 if b < full else spare):
+            total = None
+            for t, tile in enumerate(tiles):
+                term = wide[group, position, 8 * b + i, 8 * t : 8 * t + 8, :] * tile
+                total = term if total is None else total + term
+            parts.append(total)
+        value = fold(parts)
+        if b == full:
+            value = value + pltpu.roll(value, 4, axis=0)
+        rows.append(value + add[b])
+    return rows
+
+
 def fused_kernel(
-    n_circ, n_span, elem_ref, send_ref, recv_ref, count_ref, inv_hbm, coup_hbm, out_ref,
-    inv, coup, wide, line_rows, forcing, solved, state, inbox, pick_send, pick_recv, sent, arrived, back_sent, back_arrived,
+    n_circ, n_span, groups, elem_ref, send_ref, recv_ref, count_ref, inv_hbm, coup_hbm, out_ref,
+    inv, coup, wide, line_rows, forcing, parts_in, solved, inbox, outbox, pick_send, pick_recv, sent, arrived, back_sent, back_arrived,
     inv_sem, coup_sem, send_sem, recv_sem, go_send, go_recv, back_send, back_recv,
 ):
     circ, span = lax.axis_index("circ"), lax.axis_index("span")
@@ -301,7 +409,12 @@
             )
 
         def start(o, _):
-            copy(lax.rem(me + o, peers), me).start()
+            peer = o // n_span * n_span + lax.rem(span + o, n_span)
+
+            @pl.when(peer != me)
+            def _():
+                copy(peer, me).start()
+
             return 0
 
         def land(o, _):
@@ -314,7 +427,7 @@
             return 0
 
         return (
-            lambda: lax.fori_loop(1, peers, start, 0),
+            lambda: lax.fori_loop(0, peers, start, 0),
             lambda: lax.fori_loop(1, peers, land, 0),
             lambda: lax.fori_loop(1, peers, drain, 0),
         )
@@ -331,15 +444,30 @@
     start()
     arrived[me] = sent[me]
     build(recv_ref, pick_recv, True)
+    full, spare = row_plan(width, groups)
     for k in range(segment):
         coup_loads[k].wait()
 
-        def widen(b, _, k=k):
-            for i in range(8):
-                wide[k, b * 8 + i] = coup[k, b * 8 + i].astype(jnp.float32)
-            return 0
-
-        lax.fori_loop(0, blocks, widen, 0)
+        def widen(row, _, k=k):
+            first = row // 8 * (8 * groups) + lax.rem(row, 8)
+            for start in range(0, width, 16):
+                pieces = [coup[k, first + 8 * a, start : start + 16, :].astype(jnp.float32) for a in range(groups)]
+                for g, piece in enumerate(turn_lanes(pieces)):
+                    wide[g, k, row, start : start + 16, :] = piece
+            return 0
+
+        lax.fori_loop(0, 8 * full, widen, 0)
+
+        def widen_spare(row, _, k=k):
+            first = 8 * full * groups + row
+            for start in range(0, width, 16):
+                pieces = [coup[k, first + spare * a, start : start + 16, :].astype(jnp.float32) for a in range(groups)]
+                for g, piece in enumerate(turn_lanes(pieces)):
+                    wide[g, k, 8 * full + row, start : start + 16, :] = piece
+            return 0
+
+        if spare:
+            lax.fori_loop(0, spare, widen_spare, 0)
     land()
 
     def turned(block):
@@ -368,63 +496,63 @@
 
         lax.fori_loop(0, blocks, force, 0)
 
-    cut = (blocks // 4) * 16
-    chunks = ((0, cut), (cut, width))
-
-    def hop(turn, slot, chunk):
-        rows = pl.ds(chunks[chunk][0], chunks[chunk][1] - chunks[chunk][0])
+    held = full + (spare > 0)
+    for k in range(segment):
+        packed = to_groups([forcing[k, 8 * b : 8 * b + 8, :] for b in range(blocks)], groups)
+        for g in range(groups):
+            for b in range(held):
+                parts_in[g, k, 8 * b : 8 * b + 8, :] = packed[g][b]
+
+    @pl.when(circ == 0)
+    def _():
+        inbox[0] = jnp.zeros_like(inbox[0])
+
+    def hop(turn, slot, group):
         return pltpu.make_async_remote_copy(
-            src_ref=solved.at[segment - 1, rows],
-            dst_ref=inbox.at[slot, rows],
-            send_sem=send_sem.at[turn, chunk],
-            recv_sem=recv_sem.at[slot, chunk],
+            src_ref=outbox.at[turn, group],
+            dst_ref=inbox.at[slot, group],
+            send_sem=send_sem.at[turn, group],
+            recv_sem=recv_sem.at[slot, group],
             device_id={"circ": right},
             device_id_type=MESH,
         )
 
-    def sweep(emit):
+    def visit(order, _):
+        turn, group = order // groups, lax.rem(order, groups)
+
+        @pl.when(circ + turn > 0)
+        def _():
+            hop(0, turn, group).wait_recv()
+
+        rows = [inbox[turn, group, 8 * b : 8 * b + 8, :] for b in range(held)]
         for k in range(segment):
-            vector = state[...] if k == 0 else solved[k - 1]
-
-            def advance(b, _, k=k, vector=vector):
-                for base in (pl.multiple_of(b * 16, 16), pl.multiple_of(b * 16 + 8, 8)):
-                    rows = block_rows(wide, k, base, vector)
-                    solved[k, pl.ds(base, 8), :] = forcing[k, pl.ds(base, 8), :] + rows
-                return 0
-
-            if k < segment - 1:
-                lax.fori_loop(0, blocks // 2, advance, 0)
-            else:
-                for chunk in range(2):
-                    lax.fori_loop(chunks[chunk][0] // 16, chunks[chunk][1] // 16, advance, 0)
-                    emit(chunk)
-
-    @pl.when(circ == 0)
-    def _():
-        state[...] = jnp.zeros_like(state)
-
-    @pl.when(circ > 0)
-    def _():
-        for chunk in range(2):
-            hop(0, 0, chunk).wait_recv()
-        state[...] = inbox[0]
-
-    landing = jnp.where(circ == n_circ - 1, 1, 0)
-    sweep(lambda chunk: hop(0, landing, chunk).start())
-    for chunk in range(2):
-        hop(0, 1, chunk).wait_send()
-    for chunk in range(2):
-        hop(0, 1, chunk).wait_recv()
-    state[...] = inbox[1]
-
-    def last(chunk):
-        @pl.when(circ < n_circ - 1)
+            add = [parts_in[group, k, 8 * b : 8 * b + 8, :] for b in range(held)]
+            rows = advance(wide, group, k, replicate(rows, width, groups), add, width, groups)
+            for b in range(held):
+                solved[group, k, 8 * b : 8 * b + 8, :] = rows[b]
+        for b in range(held):
+            outbox[turn, group, 8 * b : 8 * b + 8, :] = rows[b]
+
+        @pl.when(circ + turn < n_circ)
         def _():
-            hop(1, 1, chunk).start()
-
-    sweep(last)
-
-    table = jnp.concatenate([solved[k] for k in range(segment)], axis=1)
+            hop(turn, jnp.where(circ == n_circ - 1, 1, turn), group).start()
+
+        return 0
+
+    lax.fori_loop(0, 2 * groups, visit, 0)
+
+    table = jnp.concatenate(
+        [
+            jnp.concatenate(
+                from_groups(
+                    [[solved[g, k, 8 * b : 8 * b + 8, :] for b in range(held)] for g in range(groups)], width
+                ),
+                axis=0,
+            )
+            for k in range(segment)
+        ],
+        axis=1,
+    )
     whole, low, high = [jnp.concatenate(split(w), axis=0) for w in spread(table)]
 
     def both(picked):
@@ -448,11 +576,16 @@
     total = sum(nn(jnp.concatenate(split(parts[t]), axis=0), pick_send[t]) for t in range(3))
     out_ref[...] = total[:width] + total[width:]
 
-    @pl.when(circ < n_circ - 1)
-    def _():
-        for chunk in range(2):
-            hop(1, 1, chunk).wait_send()
-
+    def sent_on(order, _):
+        turn, group = order // groups, lax.rem(order, groups)
+
+        @pl.when(circ + turn < n_circ)
+        def _():
+            hop(turn, 0, group).wait_send()
+
+        return 0
+
+    lax.fori_loop(0, 2 * groups, sent_on, 0)
     drain_go()
     drain_back()
 
@@ -464,25 +597,29 @@
     third = slots // 3
     vmem = pl.BlockSpec(memory_space=pltpu.VMEM)
     hbm = pl.BlockSpec(memory_space=pl.ANY)
-    boxes = pltpu.VMEM((2, width, lines), jnp.float32)
-    states = pltpu.VMEM((segment, width, lines), jnp.float32)
+    groups = GROUPS
+    full, spare = row_plan(width, groups)
+    rows = 8 * (full + (spare > 0))
+    boxes = pltpu.VMEM((2, groups, rows, lines), jnp.float32)
+    packed = pltpu.VMEM((groups, segment, rows, lines), jnp.float32)
     pick = pltpu.VMEM((3, peers * third, segment * lines), jnp.bfloat16)
     go = pltpu.VMEM((peers, 2 * third, 128), jnp.bfloat16)
     back = pltpu.VMEM((peers, 2 * third, 128), jnp.int16)
     dma = pltpu.SemaphoreType.DMA
     return pl.pallas_call(
-        functools.partial(fused_kernel, n_circ, n_span),
+        functools.partial(fused_kernel, n_circ, n_span, groups),
         out_shape=jax.ShapeDtypeStruct(elem_rows.shape, jnp.float32),
         in_specs=[vmem, vmem, vmem, vmem, hbm, hbm],
         out_specs=vmem,
         scratch_shapes=[
             pltpu.VMEM(inverses.shape, jnp.bfloat16),
             pltpu.VMEM(coupling.shape, jnp.bfloat16),
-            pltpu.VMEM(coupling.shape, jnp.float32),
+            pltpu.VMEM((groups, segment, 8 * full + spare, width, lines), jnp.float32),
             pltpu.VMEM((segment, width, lines), jnp.bfloat16),
-            states,
-            states,
-            pltpu.VMEM((width, lines), jnp.float32),
+            pltpu.VMEM((segment, width, lines), jnp.float32),
+            packed,
+            packed,
+            boxes,
             boxes,
             pick,
             pick,
@@ -492,8 +629,8 @@
             back,
             dma((segment,)),
             dma((segment,)),
-            dma((2, 2)),
-            dma((2, 2)),
+            dma((2, groups)),
+            dma((2, groups)),
             dma((peers,)),
             dma((peers,)),
             dma((peers,)),

time: 65.7 us -> 81.9 us (1.25)
  Pallas kernels: 63.9 us -> 80 us
    pallas_call x1, Pallas kernels: 63.9 us -> 80 us  [fused(): pl.pallas_call(functools.partial(fused_kernel, n_circ, n_span, groups), o...]
where the time goes in v1:
time: 81.9 us; the launch traced here: 81.7 us
  Pallas kernels  80 us (98%)
  local copies, waits for them, and re-layouts  1.65 us (2%)
    pallas_call x1, Pallas kernels, fused(): pl.pallas_call(functools.partial(fused_kernel, n_circ, n_span, groups), o...  80 us
    unnamed x1, local copies, waits for them, and re-layouts  1.65 us

profile of v1, /device:TPU:0, one launch (start us, length us, event | category | flops | bytes accessed | tf_op | source)
XLA Modules:
  0.0 81.7 jit_solution(14569246999213206537)
XLA Ops:
  0.0 80.0 %smooth.1 = f32[80,768]{1,0:T(8,128)} custom-call(bf16[80,768]{1,0:T(8,128)(2,1)} %elem_ref.1, s32[32,48]{1,0:T(8,128)} %bitcast.2, s32[32,48]{1,0:T(8,128)} %bitcast.3, s32[1,32]{1,0:T(1,128)} %count_ref.1, bf16[6,80,80,128]{3,2,1,0:T(8,128)(2,1)} %inv_hbm.1, bf16[6,80,80,128]{3,2,1,0:T(8,128)(2,1)} %coup_hbm.1), custom_call_target="tpu_custom_call" | custom-call | tf_op jit(solution)/shard_map/smooth/pallas_call | solution.py:609
  80.1 1.7 %copy.8 = f32[80,768]{1,0:T(8,128)} copy(f32[80,768]{1,0:T(8,128)} %smooth.1) | data formatting | bytes 491520

commit v2 on v0

--- a/solution.py
+++ b/solution.py
@@ -236,9 +236,45 @@
     )
 
 
+def flip_block(source, target, flat, position, block):
+    width = source.shape[2]
+    for i in range(16):
+        for start in range(0, width, 16):
+            piece = source[position, block * 16 + i, start : start + 16, :].astype(jnp.float32)
+            flat[(width + 8) * i + start : (width + 8) * i + start + 16, :] = piece
+    rows = pl.ds(pl.multiple_of(block * 16, 16), 16)
+    for j in range(width):
+        target[position, j, rows, :] = flat[pl.ds(j, 16, stride=width + 8), :].astype(jnp.bfloat16)
+
+
+def columns(matrix, position, planes, spots):
+    width, count = planes.shape[1], planes.shape[0]
+
+    def run(tile, first, last):
+        total = None
+        for j in range(first, last):
+            for p in range(count):
+                spot = spots[p, j].astype(jnp.float32)
+                term = matrix[position, j, 16 * tile : 16 * tile + 16, :].astype(jnp.float32) * spot
+                total = term if total is None else total + term
+        return total
+
+    for j in range(width):
+        for p in range(count):
+            spots[p, j] = jnp.broadcast_to(planes[p, j : j + 1, :], (16, planes.shape[2])).astype(jnp.bfloat16)
+    tiles = width // 16
+    whole = tiles // 4 * 4
+    totals = [run(tile, 0, width) for tile in range(whole)]
+    for tile in range(whole, tiles):
+        cuts = [width * q // 4 for q in range(5)]
+        quarters = [run(tile, cuts[q], cuts[q + 1]) for q in range(4)]
+        totals.append((quarters[0] + quarters[1]) + (quarters[2] + quarters[3]))
+    return jnp.concatenate(totals, axis=0)
+
+
 def fused_kernel(
     n_circ, n_span, elem_ref, send_ref, recv_ref, count_ref, inv_hbm, coup_hbm, out_ref,
-    inv, coup, wide, line_rows, forcing, solved, state, inbox, pick_send, pick_recv, sent, arrived, back_sent, back_arrived,
+    inv, coup, wide, flat, planes, spots, line_rows, forcing, solved, state, inbox, pick_send, pick_recv, sent, arrived, back_sent, back_arrived,
     inv_sem, coup_sem, send_sem, recv_sem, go_send, go_recv, back_send, back_recv,
 ):
     circ, span = lax.axis_index("circ"), lax.axis_index("span")
@@ -335,11 +371,10 @@
         coup_loads[k].wait()
 
         def widen(b, _, k=k):
-            for i in range(8):
-                wide[k, b * 8 + i] = coup[k, b * 8 + i].astype(jnp.float32)
-            return 0
-
-        lax.fori_loop(0, blocks, widen, 0)
+            flip_block(coup, wide, flat, k, b)
+            return 0
+
+        lax.fori_loop(0, width // 16, widen, 0)
     land()
 
     def turned(block):
@@ -383,21 +418,15 @@
         )
 
     def sweep(emit):
+        value = state[...]
         for k in range(segment):
-            vector = state[...] if k == 0 else solved[k - 1]
-
-            def advance(b, _, k=k, vector=vector):
-                for base in (pl.multiple_of(b * 16, 16), pl.multiple_of(b * 16 + 8, 8)):
-                    rows = block_rows(wide, k, base, vector)
-                    solved[k, pl.ds(base, 8), :] = forcing[k, pl.ds(base, 8), :] + rows
-                return 0
-
-            if k < segment - 1:
-                lax.fori_loop(0, blocks // 2, advance, 0)
-            else:
-                for chunk in range(2):
-                    lax.fori_loop(chunks[chunk][0] // 16, chunks[chunk][1] // 16, advance, 0)
-                    emit(chunk)
+            high, low = split(value)
+            planes[0] = high.astype(jnp.float32)
+            planes[1] = low.astype(jnp.float32)
+            value = forcing[k] + columns(wide, k, planes, spots)
+            solved[k] = value
+        for chunk in range(2):
+            emit(chunk)
 
     @pl.when(circ == 0)
     def _():
@@ -478,7 +507,10 @@
         scratch_shapes=[
             pltpu.VMEM(inverses.shape, jnp.bfloat16),
             pltpu.VMEM(coupling.shape, jnp.bfloat16),
-            pltpu.VMEM(coupling.shape, jnp.float32),
+            pltpu.VMEM(coupling.shape, jnp.bfloat16),
+            pltpu.VMEM((16 * (width + 8), lines), jnp.float32),
+            pltpu.VMEM((2, width, lines), jnp.float32),
+            pltpu.VMEM((2, width, 16, lines), jnp.bfloat16),
             pltpu.VMEM((segment, width, lines), jnp.bfloat16),
             states,
             states,

time: 65.7 us -> 61.3 us (0.933)
  Pallas kernels: 63.9 us -> 59.5 us
    pallas_call x1, Pallas kernels: 63.9 us -> 59.5 us  [fused(): pl.pallas_call(functools.partial(fused_kernel, n_circ, n_span), out_shape...]
where the time goes in v2:
time: 61.3 us; the launch traced here: 61.1 us
  Pallas kernels  59.5 us (97%)
  local copies, waits for them, and re-layouts  1.65 us (3%)
    pallas_call x1, Pallas kernels, fused(): pl.pallas_call(functools.partial(fused_kernel, n_circ, n_span), out_shape...  59.5 us
    unnamed x1, local copies, waits for them, and re-layouts  1.65 us

profile of v2, /device:TPU:0, one launch (start us, length us, event | category | flops | bytes accessed | tf_op | source)
XLA Modules:
  0.0 61.1 jit_solution(4507496576826678875)
XLA Ops:
  0.0 59.5 %smooth.1 = f32[80,768]{1,0:T(8,128)} custom-call(bf16[80,768]{1,0:T(8,128)(2,1)} %elem_ref.1, s32[32,48]{1,0:T(8,128)} %bitcast.2, s32[32,48]{1,0:T(8,128)} %bitcast.3, s32[1,32]{1,0:T(1,128)} %count_ref.1, bf16[6,80,80,128]{3,2,1,0:T(8,128)(2,1)} %inv_hbm.1, bf16[6,80,80,128]{3,2,1,0:T(8,128)(2,1)} %coup_hbm.1), custom_call_target="tpu_custom_call" | custom-call | tf_op jit(solution)/shard_map/smooth/pallas_call | solution.py:502
  59.5 1.7 %copy.8 = f32[80,768]{1,0:T(8,128)} copy(f32[80,768]{1,0:T(8,128)} %smooth.1) | data formatting | bytes 491520

commit v3 on v2

--- a/solution.py
+++ b/solution.py
@@ -189,26 +189,29 @@
     )
 
 
-def code(values, lane, width, extra):
-    size = jnp.abs(values)
-    tiny = jnp.float32(1e-36)
-    top_main = jnp.max(jnp.where(lane < width, size, tiny), axis=1, keepdims=True)
-    top_extra = jnp.max(jnp.where(lane < width, tiny, size), axis=1, keepdims=True)
-    power_main = jnp.ceil(jnp.log2(jnp.maximum(top_main, tiny)))
-    power_extra = jnp.ceil(jnp.log2(jnp.maximum(top_extra, tiny)))
-    root = jnp.exp2(-0.5 * jnp.where(lane < width, power_main, power_extra))
-    whole = jnp.round(values * root * root * 32000.0)
-    whole = jnp.where(lane == width + extra, power_main, whole)
-    whole = jnp.where(lane == width + extra + 1, power_extra, whole)
-    return whole.astype(jnp.int32).astype(jnp.int16)
-
-
-def decode(coded, lane, width, extra):
-    whole = coded.astype(jnp.int32).astype(jnp.float32)
-    power_main = jnp.sum(jnp.where(lane == width + extra, whole, 0.0), axis=1, keepdims=True)
-    power_extra = jnp.sum(jnp.where(lane == width + extra + 1, whole, 0.0), axis=1, keepdims=True)
-    root = jnp.exp2(0.5 * jnp.where(lane < width, power_main, power_extra))
-    return jnp.where(lane < width + extra, whole * (1.0 / 32000.0) * root * root, 0.0)
+def code(table):
+    top = jnp.max(jnp.abs(table), axis=0, keepdims=True)
+    power = jnp.ceil(jnp.log2(jnp.maximum(top, jnp.float32(1e-36))))
+    root = jnp.exp2(-0.5 * power)
+    whole = jnp.round(table * root * root * 32000.0)
+    upper = jnp.round(whole * (1.0 / 256.0))
+    return upper, whole - 256.0 * upper, power
+
+
+def placed(table, power):
+    parts = spread(table)
+    width, cells = table.shape
+    start = width + width // 2
+    row = lax.broadcasted_iota(jnp.int32, (8, cells), 0)
+    marks = [jnp.where(row == spot, power, 0.0) for spot in (0, 1, 1)]
+    return [jnp.concatenate([part[:start], mark], axis=0) for part, mark in zip(parts, marks)]
+
+
+def decode(whole, marks, spot):
+    upper = jnp.round(whole * (1.0 / 256.0))
+    row = lax.broadcasted_iota(jnp.int32, marks.shape, 0)
+    power = jnp.where(row == spot, marks, 0.0)
+    return jnp.concatenate([upper, whole - 256.0 * upper, power, jnp.zeros_like(power)], axis=0).astype(jnp.bfloat16)
 
 
 def split(values):
@@ -454,28 +457,35 @@
     sweep(last)
 
     table = jnp.concatenate([solved[k] for k in range(segment)], axis=1)
-    whole, low, high = [jnp.concatenate(split(w), axis=0) for w in spread(table)]
+    upper, lower, power = code(table)
+    whole, low, high = [
+        jnp.concatenate([u, v], axis=0).astype(jnp.bfloat16)
+        for u, v in zip(placed(upper, jnp.zeros_like(power)), placed(lower, power))
+    ]
 
     def both(picked):
-        return picked[:, :128] + picked[:, 128:]
-
-    lane = lax.broadcasted_iota(jnp.int32, (peers * third, 128), 1)
+        return (256.0 * picked[:, :128] + picked[:, 128:]).astype(jnp.int32).astype(jnp.int16)
+
     first = both(nt(pick_recv[0], whole) + nt(pick_recv[2], low))
     second = both(nt(pick_recv[1], whole) + nt(pick_recv[2], high))
-    back_sent[:, :third, :] = code(first, lane, width, half).reshape(peers, third, 128)
-    back_sent[:, third:, :] = code(second, lane, width, half).reshape(peers, third, 128)
+    back_sent[:, :third, :] = first.reshape(peers, third, 128)
+    back_sent[:, third:, :] = second.reshape(peers, third, 128)
     start, land, drain_back = exchange(back_sent, back_arrived, back_send, back_recv)
     start()
     back_arrived[me] = back_sent[me]
     land()
 
     def opened(block):
-        return jnp.transpose(decode(block.reshape(peers * third, 128), lane, width, half))
+        return jnp.transpose(block.reshape(peers * third, 128).astype(jnp.int32).astype(jnp.float32))
 
     first, second = opened(back_arrived[:, :third, :]), opened(back_arrived[:, third:, :])
     parts, _ = collect(first, second, pick_send)
-    total = sum(nn(jnp.concatenate(split(parts[t]), axis=0), pick_send[t]) for t in range(3))
-    out_ref[...] = total[:width] + total[width:]
+    tail = width + half
+    marks = (first[tail : tail + 8], second[tail : tail + 8], first[tail : tail + 8])
+    total = sum(nn(decode(parts[t], marks[t], t // 2), pick_send[t]) for t in range(3))
+    power = total[2 * width : 2 * width + 1] + total[2 * width + 1 : 2 * width + 2]
+    root = jnp.exp2(0.5 * power)
+    out_ref[...] = (256.0 * total[:width] + total[width : 2 * width]) * (1.0 / 32000.0) * root * root
 
     @pl.when(circ < n_circ - 1)
     def _():
@@ -539,7 +549,7 @@
 
 
 def packs(width, slots, cells, lines):
-    return slots % 48 == 0 and width % 16 == 0 and width + width // 2 + 2 <= 128 and lines == 128
+    return slots % 48 == 0 and width % 16 == 0 and width + width // 2 + 8 == 128 and lines == 128
 
 
 def local(*arrays):

time: 61.3 us -> 60.9 us (level)
  no operation moved by 1% of the time
where the time goes in v3:
time: 60.9 us; the launch traced here: 60.8 us
  Pallas kernels  59.1 us (97%)
  local copies, waits for them, and re-layouts  1.65 us (3%)
    pallas_call x1, Pallas kernels, fused(): pl.pallas_call(functools.partial(fused_kernel, n_circ, n_span), out_shape...  59.1 us
    unnamed x1, local copies, waits for them, and re-layouts  1.65 us

profile of v3, /device:TPU:0, one launch (start us, length us, event | category | flops | bytes accessed | tf_op | source)
XLA Modules:
  0.0 60.8 jit_solution(15312352184051809407)
XLA Ops:
  0.0 59.1 %smooth.1 = f32[80,768]{1,0:T(8,128)} custom-call(bf16[80,768]{1,0:T(8,128)(2,1)} %elem_ref.1, s32[32,48]{1,0:T(8,128)} %bitcast.2, s32[32,48]{1,0:T(8,128)} %bitcast.3, s32[1,32]{1,0:T(1,128)} %count_ref.1, bf16[6,80,80,128]{3,2,1,0:T(8,128)(2,1)} %inv_hbm.1, bf16[6,80,80,128]{3,2,1,0:T(8,128)(2,1)} %coup_hbm.1), custom_call_target="tpu_custom_call" | custom-call | tf_op jit(solution)/shard_map/smooth/pallas_call | solution.py:512
  59.1 1.7 %copy.8 = f32[80,768]{1,0:T(8,128)} copy(f32[80,768]{1,0:T(8,128)} %smooth.1) | data formatting | bytes 491520

commit v4 on v3

--- a/solution.py
+++ b/solution.py
@@ -292,9 +292,6 @@
 
     coup_loads = [pltpu.make_async_copy(coup_hbm.at[k], coup.at[k], coup_sem.at[k]) for k in range(segment)]
     inv_loads = [pltpu.make_async_copy(inv_hbm.at[k], inv.at[k], inv_sem.at[k]) for k in range(segment)]
-    for load in coup_loads + inv_loads:
-        load.start()
-
     barrier = pltpu.get_barrier_semaphore()
 
     def greet(o, _):
@@ -305,6 +302,9 @@
         return 0
 
     lax.fori_loop(1, peers, greet, 0)
+
+    for load in coup_loads + inv_loads:
+        load.start()
 
     def build(index_ref, pick, masked):
         lane = lax.broadcasted_iota(jnp.int32, (third, index_ref.shape[1]), 1)
@@ -400,11 +400,11 @@
         vector = line_rows[k].astype(jnp.float32)
 
         def force(b, _, k=k, vector=vector):
-            base = pl.multiple_of(b * 8, 8)
-            forcing[k, pl.ds(base, 8), :] = block_rows(inv, k, base, vector)
-            return 0
-
-        lax.fori_loop(0, blocks, force, 0)
+            for base in (pl.multiple_of(b * 16, 16), pl.multiple_of(b * 16 + 8, 8)):
+                forcing[k, pl.ds(base, 8), :] = block_rows(inv, k, base, vector)
+            return 0
+
+        lax.fori_loop(0, blocks // 2, force, 0)
 
     cut = (blocks // 4) * 16
     chunks = ((0, cut), (cut, width))

time: 60.9 us -> 60.4 us (level)
  no operation moved by 1% of the time
where the time goes in v4:
time: 60.4 us; the launch traced here: 60.2 us
  Pallas kernels  58.6 us (97%)
  local copies, waits for them, and re-layouts  1.65 us (3%)
    pallas_call x1, Pallas kernels, fused(): pl.pallas_call(functools.partial(fused_kernel, n_circ, n_span), out_shape...  58.6 us
    unnamed x1, local copies, waits for them, and re-layouts  1.65 us

profile of v4, /device:TPU:0, one launch (start us, length us, event | category | flops | bytes accessed | tf_op | source)
XLA Modules:
  0.0 60.2 jit_solution(926685294923372345)
XLA Ops:
  0.0 58.6 %smooth.1 = f32[80,768]{1,0:T(8,128)} custom-call(bf16[80,768]{1,0:T(8,128)(2,1)} %elem_ref.1, s32[32,48]{1,0:T(8,128)} %bitcast.2, s32[32,48]{1,0:T(8,128)} %bitcast.3, s32[1,32]{1,0:T(1,128)} %count_ref.1, bf16[6,80,80,128]{3,2,1,0:T(8,128)(2,1)} %inv_hbm.1, bf16[6,80,80,128]{3,2,1,0:T(8,128)(2,1)} %coup_hbm.1), custom_call_target="tpu_custom_call" | custom-call | tf_op jit(solution)/shard_map/smooth/pallas_call | solution.py:512
  58.6 1.7 %copy.8 = f32[80,768]{1,0:T(8,128)} copy(f32[80,768]{1,0:T(8,128)} %smooth.1) | data formatting | bytes 491520
